TPU v7x, 128 devices: a whole 4x4x4 slice. The times are simulated.
128 devices in a mesh: seq: 32 (over x, y_hi, z), head: 4 (over y_lo, core).
Axes of the slice: x: 4, y: 4 (y_hi: 2, y_lo: 2; y = y_hi * 2 + y_lo), z: 4, core: 2. Of those that a mesh axis runs over, the one named last changes fastest.
Arguments:
- queries: bfloat16 [2, 16384, 4096], P(None, ('seq', 'head')), may hold values from -6 to 6
- memory_keys: bfloat16 [2, 16384, 4096], P(None, ('seq', 'head')), may hold values from -6 to 6
- memory_values: bfloat16 [2, 16384, 4096], P(None, ('seq', 'head')), may hold values from -6 to 6
- rates: float32 [2, 16384, 8], P(None, ('seq', 'head')), may hold values from 0.001 to 0.01
- fast_gate: float32 [8, 512, 512], P('head'), may hold values from -0.25 to 0.25
- fast_up: float32 [8, 512, 512], P('head'), may hold values from -0.25 to 0.25
- fast_down: float32 [8, 512, 512], P('head'), may hold values from -0.25 to 0.25
Outputs:
- outputs: bfloat16 [2, 16384, 4096], P(None, ('seq', 'head'))
- final_gate: float32 [8, 512, 512], P('head')
- final_up: float32 [8, 512, 512], P('head')
- final_down: float32 [8, 512, 512], P('head')
All inputs are finite; a program needn't handle non-finite values.
Results may differ from a plain program's by a relative error of at most 0.035.
Values may be sent and summed in bfloat16 or wider, within the bound.
A program may use at most 128 MiB of HBM per device.

v0:
```python
import jax
import jax.numpy as jnp
from jax import lax
from jax.sharding import PartitionSpec as P

EPSILON = 1e-06


def side_by_side(arrays, axis, dim, along):
    both = jnp.concatenate(arrays, axis=along)
    out, at, gathered = (lax.psum_scatter(both, axis, scatter_dimension=dim, tiled=True), 0, [])
    for a in arrays:
        gathered.append(lax.slice_in_dim(out, at, at + a.shape[along], axis=along))
        at += a.shape[along]
    return tuple(gathered)


def rows_first(arrays, axis, dims):
    turned = [jnp.moveaxis(a, dim, 0) for a, dim in zip(arrays, dims)]
    widths = [t[0].size for t in turned]
    both = jnp.concatenate([t.reshape(-1, w) for t, w in zip(turned, widths)], axis=1)
    out = lax.all_gather(both, axis, axis=0, tiled=True)
    parts = jnp.split(out, [sum(widths[:k]) for k in range(1, len(widths))], axis=1)
    return tuple(
        (
            jnp.moveaxis(b.reshape(-1, *t.shape[1:]), 0, dim)
            for b, t, dim in zip(parts, turned, dims)
        )
    )


def head_gradients(gate_weight, up_weight, down_weight, key_block, value_block, rate_block):
    gate_half = gate_weight.astype(jnp.bfloat16)
    up_half = up_weight.astype(jnp.bfloat16)
    down_half = down_weight.astype(jnp.bfloat16)
    gate_pre = jnp.dot(key_block, gate_half, preferred_element_type=jnp.float32)
    up_pre = jnp.dot(key_block, up_half, preferred_element_type=jnp.float32)
    sigmoid_gate = jax.nn.sigmoid(gate_pre)
    activated = gate_pre * sigmoid_gate
    hidden = (activated * up_pre).astype(jnp.bfloat16)
    target = (-rate_block[:, None] * value_block.astype(jnp.float32)).astype(jnp.bfloat16)
    grad_down = jnp.dot(hidden.T, target, preferred_element_type=jnp.float32)
    hidden_grad = jnp.dot(target, down_half.T, preferred_element_type=jnp.float32)
    gate_delta = (
        hidden_grad * up_pre * sigmoid_gate * (1.0 + gate_pre * (1.0 - sigmoid_gate))
    ).astype(jnp.bfloat16)
    up_delta = (hidden_grad * activated).astype(jnp.bfloat16)
    grad_gate = jnp.dot(key_block.T, gate_delta, preferred_element_type=jnp.float32)
    grad_up = jnp.dot(key_block.T, up_delta, preferred_element_type=jnp.float32)
    return (grad_gate, grad_up, grad_down)


def renormalize(weight, gradient):
    updated = weight - gradient
    old_norm = jnp.sqrt(jnp.sum(weight * weight, axis=-2, keepdims=True) + EPSILON)
    new_norm = jnp.sqrt(jnp.sum(updated * updated, axis=-2, keepdims=True) + EPSILON)
    return updated * (old_norm / new_norm)


def apply_head(gate_weight, up_weight, down_weight, query_block):
    gate_pre = jnp.dot(
        query_block, gate_weight.astype(jnp.bfloat16), preferred_element_type=jnp.float32
    )
    up_pre = jnp.dot(
        query_block, up_weight.astype(jnp.bfloat16), preferred_element_type=jnp.float32
    )
    hidden = (jax.nn.silu(gate_pre) * up_pre).astype(jnp.bfloat16)
    return jnp.dot(
        hidden, down_weight.astype(jnp.bfloat16), preferred_element_type=jnp.float32
    ).astype(jnp.bfloat16)


def on_device(queries, memory_keys, memory_values, rates, fast_gate, fast_up, fast_down):
    local_heads = fast_gate.shape[0]
    head_size = fast_gate.shape[1]
    gate_state, up_state, down_state = (fast_gate, fast_up, fast_down)
    results = []
    for block_index in range(queries.shape[0]):
        query_block, key_rows, value_rows, rate_rows = (
            lax.all_to_all(queries[block_index], "head", split_axis=1, concat_axis=0, tiled=True),
            lax.all_to_all(
                memory_keys[block_index], "head", split_axis=1, concat_axis=0, tiled=True
            ),
            lax.all_to_all(
                memory_values[block_index], "head", split_axis=1, concat_axis=0, tiled=True
            ),
            lax.all_to_all(
                rates[block_index].astype(jnp.bfloat16),
                "head",
                split_axis=1,
                concat_axis=0,
                tiled=True,
            ).astype(jnp.float32),
        )
        row_count = key_rows.shape[0]
        key_heads = key_rows.reshape(row_count, local_heads, head_size)
        value_heads = value_rows.reshape(row_count, local_heads, head_size)
        grad_gate, grad_up, grad_down = jax.vmap(head_gradients, in_axes=(0, 0, 0, 1, 1, 1))(
            gate_state, up_state, down_state, key_heads, value_heads, rate_rows
        )
        share_gate, share_up, share_down = side_by_side(
            (grad_gate, grad_up, grad_down), "seq", 2, 0
        )
        position = lax.axis_index("seq")
        wide_cols = share_gate.shape[2]
        narrow_cols = share_down.shape[2]
        gate_part = lax.dynamic_slice_in_dim(gate_state, position * wide_cols, wide_cols, 2)
        up_part = lax.dynamic_slice_in_dim(up_state, position * wide_cols, wide_cols, 2)
        down_part = lax.dynamic_slice_in_dim(down_state, position * narrow_cols, narrow_cols, 2)
        gate_state, up_state, down_state = rows_first(
            (
                renormalize(gate_part, share_gate),
                renormalize(up_part, share_up),
                renormalize(down_part, share_down),
            ),
            "seq",
            (2, 2, 2),
        )
        query_heads = query_block.reshape(row_count, local_heads, head_size)
        applied = jax.vmap(apply_head, in_axes=(0, 0, 0, 1), out_axes=1)(
            gate_state, up_state, down_state, query_heads
        )
        flattened = applied.reshape(row_count, local_heads * head_size)
        results.append(lax.all_to_all(flattened, "head", split_axis=0, concat_axis=1, tiled=True))
    return (jnp.stack(results), gate_state, up_state, down_state)


def solution(mesh):
    placed = (
        P(None, ("seq", "head"), None),
        P(None, ("seq", "head"), None),
        P(None, ("seq", "head"), None),
        P(None, ("seq", "head"), None),
        P("head", None, None),
        P("head", None, None),
        P("head", None, None),
    )
    return jax.shard_map(
        on_device,
        mesh=mesh,
        in_specs=placed,
        out_specs=(
            P(None, ("seq", "head"), None),
            P("head", None, None),
            P("head", None, None),
            P("head", None, None),
        ),
        check_vma=False,
    )
```

profile of v0, /device:TPU:1, one launch (start us, length us, event | category | flops | bytes accessed | tf_op | source)
XLA Modules:
  0.0 849.1 jit_solution(13516002695234493756)
XLA Ops:
  8.5 4.6 all-to-all-start
  17.8 3.5 all-to-all-start.2
  26.1 8.7 %all-to-all-done.2 = bf16[128,4,1024]{2,0,1:T(8,128)(2,1)S(1)} async-done(((bf16[128,4,1024]{2,0,1:T(8,128)(2,1)}), bf16[128,4,1024]{2,0,1:T(8,128)(2,1)S(1)}, u32[]{:S(2)}, u32[]{:S(2)}) %all-to-all-start.2) | async-done | bytes 1048608 | tf_op jit(solution)/shard_map/all_to_all | solution.py:81
  34.8 5.2 all-to-all-start.1
  42.2 3.8 fusion.45
  48.2 5.4 all-to-all-done.1
  57.8 3.2 fusion.47
  66.2 3.4 pad_maximum_fusion
  72.9 235.8 %reduce-scatter.3.cloned.1.call-done = f32[6,512,16]{1,2,0:T(8,128)} async-done(((f32[6,512,512]{1,2,0:T(8,128)}), f32[6,512,16]{1,2,0:T(8,128)}) %reduce-scatter.3.cloned.1.call-update) | async-done | bytes 196624 | tf_op jit(solution)/shard_map/reduce_scatter | solution.py:11
  311.5 6.3 all-to-all-start.5
  320.8 4.3 all-to-all-start.7
  327.2 11.5 %all-to-all-done.7 = bf16[128,4,1024]{2,0,1:T(8,128)(2,1)S(1)} async-done(((bf16[128,4,1024]{2,0,1:T(8,128)(2,1)}), bf16[128,4,1024]{2,0,1:T(8,128)(2,1)S(1)}, u32[]{:S(2)}, u32[]{:S(2)}) %all-to-all-start.7) | async-done | bytes 1048608 | tf_op jit(solution)/shard_map/all_to_all | solution.py:81
  338.7 5.1 all-to-all-start.6
  346.0 17.0 %all-to-all-done.6 = bf16[128,4,1024]{2,0,1:T(8,128)(2,1)} async-done(((bf16[128,4,1024]{2,0,1:T(8,128)(2,1)}), bf16[128,4,1024]{2,0,1:T(8,128)(2,1)}, u32[]{:S(2)}, u32[]{:S(2)}) %all-to-all-start.6) | async-done | bytes 1048608 | tf_op jit(solution)/shard_map/all_to_all | solution.py:84
  367.3 42.5 %all-gather.3.cloned.1.call-done = f32[512,3072]{1,0:T(8,128)} async-done(((f32[16,3072]{1,0:T(8,128)}), f32[512,3072]{1,0:T(8,128)}) %all-gather.3.cloned.1.call-update) | async-done | bytes 6291472 | tf_op jit(solution)/shard_map/all_gather | solution.py:22
  409.7 5.8 fusion.81
  425.0 3.7 fusion.30
  433.7 3.2 fusion.27
  442.1 3.4 pad_maximum_fusion.1
  447.1 233.0 %reduce-scatter.5.cloned.1.call-done = f32[6,512,16]{1,2,0:T(8,128)} async-done(((f32[6,512,512]{1,2,0:T(8,128)}), f32[6,512,16]{1,2,0:T(8,128)}) %reduce-scatter.5.cloned.1.call-update) | async-done | bytes 196624 | tf_op jit(solution)/shard_map/reduce_scatter | solution.py:11
  689.3 6.5 all-to-all-start.8
  700.9 8.4 all-to-all-done.8
  709.3 5.1 all-to-all-start.3
  716.0 18.0 %all-to-all-done.3 = bf16[128,4,1024]{2,0,1:T(8,128)(2,1)} async-done(((bf16[128,4,1024]{2,0,1:T(8,128)(2,1)}), bf16[128,4,1024]{2,0,1:T(8,128)(2,1)}, u32[]{:S(2)}, u32[]{:S(2)}) %all-to-all-start.3) | async-done | bytes 1048608 | tf_op jit(solution)/shard_map/all_to_all | solution.py:80
  737.9 4.2 fusion.19
  744.8 4.3 all-to-all-start.4
  749.0 42.9 %all-gather.5.cloned.1.call-done = f32[512,3072]{1,0:T(8,128)} async-done(((f32[16,3072]{1,0:T(8,128)}), f32[512,3072]{1,0:T(8,128)}) %all-gather.5.cloned.1.call-update) | async-done | bytes 6291472 | tf_op jit(solution)/shard_map/all_gather | solution.py:22
  791.9 5.8 fusion.80
  801.3 3.6 fusion.24
  811.5 4.3 fusion.20
  818.4 4.9 all-to-all-start.9
  824.5 12.2 %all-to-all-done.9 = bf16[4,128,1024]{2,1,0:T(8,128)(2,1)S(1)} async-done(((bf16[4,128,1024]{2,1,0:T(8,128)(2,1)}), bf16[4,128,1024]{2,1,0:T(8,128)(2,1)S(1)}, u32[]{:S(2)}, u32[]{:S(2)}) %all-to-all-start.9) | async-done | bytes 1048608 | tf_op jit(solution)/shard_map/all_to_all | solution.py:124
  (116 shorter events, 105.2 us)
Async XLA Ops:
  8.5 9.3 %all-to-all-start = ((bf16[128,4,2]{0,2,1:T(2,128)(2,1)}), bf16[128,4,2]{0,2,1:T(2,128)(2,1)S(1)}, u32[]{:S(2)}, u32[]{:S(2)}) async-start(bf16[128,4,2]{0,2,1:T(2,128)(2,1)} %bitcast), calls=%async_computation | async-start | bytes 4096 | tf_op jit(solution)/shard_map/all_to_all | solution.py:87
  17.8 17.0 %all-to-all-start.2 = ((bf16[128,4,1024]{2,0,1:T(8,128)(2,1)}), bf16[128,4,1024]{2,0,1:T(8,128)(2,1)S(1)}, u32[]{:S(2)}, u32[]{:S(2)}) async-start(bf16[128,4,1024]{2,0,1:T(8,128)(2,1)} %copy.220), calls=%async_computation.2 | async-start | bytes 2097152 | tf_op jit(solution)/shard_map/all_to_all | solution.py:81
  34.8 18.7 %all-to-all-start.1 = ((bf16[128,4,1024]{2,0,1:T(8,128)(2,1)}), bf16[128,4,1024]{2,0,1:T(8,128)(2,1)}, u32[]{:S(2)}, u32[]{:S(2)}) async-start(bf16[128,4,1024]{2,0,1:T(8,128)(2,1)} %copy.218), calls=%async_computation.1 | async-start | bytes 2097152 | tf_op jit(solution)/shard_map/all_to_all | solution.py:84
  40.0 268.8 %reduce-scatter.3.cloned.1.call-start = ((), (), s32[]{:S(2)}) async-start(), calls=%async_computation.12 | async-start | bytes 6488064 | tf_op jit(solution)/shard_map/reduce_scatter | solution.py:11
  42.2 3.8 copy-start.7
  57.8 3.2 copy-start.3
  57.8 3.5 copy-start.8
  57.8 4.1 copy-start.9
  69.6 340.2 %all-gather.3.cloned.1.call-start = ((), (), s32[]{:S(2)}) async-start(), calls=%async_computation.13 | async-start | bytes 6488064 | tf_op jit(solution)/shard_map/all_gather | solution.py:22
  72.6 245.3 %copy-start.4 = (bf16[1,128,4096]{2,1,0:T(8,128)(2,1)S(1)}, bf16[1,128,4096]{2,1,0:T(8,128)(2,1)}, u32[]{:S(2)}) copy-start(bf16[1,128,4096]{2,1,0:T(8,128)(2,1)} %get-tuple-element.46) | copy-start | bytes 3145732
  311.5 9.2 %all-to-all-start.5 = ((bf16[128,4,2]{0,2,1:T(2,128)(2,1)}), bf16[128,4,2]{0,2,1:T(2,128)(2,1)S(1)}, u32[]{:S(2)}, u32[]{:S(2)}) async-start(bf16[128,4,2]{0,2,1:T(2,128)(2,1)} %bitcast.26), calls=%async_computation.6 | async-start | bytes 4096 | tf_op jit(solution)/shard_map/all_to_all | solution.py:87
  318.7 6.5 copy-start.5
  320.8 17.9 %all-to-all-start.7 = ((bf16[128,4,1024]{2,0,1:T(8,128)(2,1)}), bf16[128,4,1024]{2,0,1:T(8,128)(2,1)S(1)}, u32[]{:S(2)}, u32[]{:S(2)}) async-start(bf16[128,4,1024]{2,0,1:T(8,128)(2,1)} %copy.248), calls=%async_computation.8 | async-start | bytes 2097152 | tf_op jit(solution)/shard_map/all_to_all | solution.py:81
  338.7 24.3 %all-to-all-start.6 = ((bf16[128,4,1024]{2,0,1:T(8,128)(2,1)}), bf16[128,4,1024]{2,0,1:T(8,128)(2,1)}, u32[]{:S(2)}, u32[]{:S(2)}) async-start(bf16[128,4,1024]{2,0,1:T(8,128)(2,1)} %copy.246), calls=%async_computation.7 | async-start | bytes 2097152 | tf_op jit(solution)/shard_map/all_to_all | solution.py:84
  343.8 336.4 %reduce-scatter.5.cloned.1.call-start = ((), (), s32[]{:S(2)}) async-start(), calls=%async_computation.14 | async-start | bytes 6488064 | tf_op jit(solution)/shard_map/reduce_scatter | solution.py:11
  433.7 3.2 copy-start.2
  433.7 3.5 copy-start.10
  433.7 4.1 copy-start.11
  445.5 346.5 %all-gather.5.cloned.1.call-start = ((), (), s32[]{:S(2)}) async-start(), calls=%async_computation.15 | async-start | bytes 6488064 | tf_op jit(solution)/shard_map/all_gather | solution.py:22
  689.3 20.0 %all-to-all-start.8 = ((bf16[128,4,1024]{2,0,1:T(8,128)(2,1)}), bf16[128,4,1024]{2,0,1:T(8,128)(2,1)S(1)}, u32[]{:S(2)}, u32[]{:S(2)}) async-start(bf16[128,4,1024]{2,0,1:T(8,128)(2,1)} %copy.265), calls=%async_computation.10 | async-start | bytes 2097152 | tf_op jit(solution)/shard_map/all_to_all | solution.py:80
  709.3 24.7 %all-to-all-start.3 = ((bf16[128,4,1024]{2,0,1:T(8,128)(2,1)}), bf16[128,4,1024]{2,0,1:T(8,128)(2,1)}, u32[]{:S(2)}, u32[]{:S(2)}) async-start(bf16[128,4,1024]{2,0,1:T(8,128)(2,1)} %copy.235), calls=%async_computation.4 | async-start | bytes 2097152 | tf_op jit(solution)/shard_map/all_to_all | solution.py:80
  744.8 73.6 %all-to-all-start.4 = ((bf16[4,128,1024]{2,1,0:T(8,128)(2,1)}), bf16[4,128,1024]{2,1,0:T(8,128)(2,1)S(1)}, u32[]{:S(2)}, u32[]{:S(2)}) async-start(bf16[4,128,1024]{2,1,0:T(8,128)(2,1)} %all_to_all.117), calls=%async_computation.5 | async-start | bytes 2097152 | tf_op jit(solution)/shard_map/all_to_all | solution.py:124
  799.7 5.3 copy-start
  806.9 4.6 copy-start.1
  818.4 18.4 %all-to-all-start.9 = ((bf16[4,128,1024]{2,1,0:T(8,128)(2,1)}), bf16[4,128,1024]{2,1,0:T(8,128)(2,1)S(1)}, u32[]{:S(2)}, u32[]{:S(2)}) async-start(bf16[4,128,1024]{2,1,0:T(8,128)(2,1)} %all_to_all.129), calls=%async_computation.11 | async-start | bytes 2097152 | tf_op jit(solution)/shard_map/all_to_all | solution.py:124
  824.5 13.5 %copy-start.6 = (bf16[128,4,1024]{0,2,1:T(8,128)(2,1)S(1)}, bf16[128,4,1024]{0,2,1:T(8,128)(2,1)}, u32[]{:S(2)}) copy-start(bf16[128,4,1024]{0,2,1:T(8,128)(2,1)} %copy.244) | copy-start | bytes 3145732
Sparse Core Ops, SparseCore 0:
  69.7 239.0 reduce-scatter.2
  312.4 97.3 all-gather.2
  445.6 234.5 reduce-scatter.4
  683.2 108.6 all-gather.4
where the time goes:
time: 859 us; the launch traced here: 849 us
  waiting for transfers between devices  636 us (74%)
  local copies, waits for them, and re-layouts  90.4 us (11%)
  starting transfers between devices  50 us (6%)
  matrix products  40.7 us (5%)
  other arithmetic  17.3 us (2%)
  between operations  14.6 us (2%)
    reduce_scatter x2, waiting for transfers between devices, side_by_side(): lax.psum_scatter(both, axis, scatter_dimension=dim, tiled=True)  469 us
    all_gather x2, waiting for transfers between devices, rows_first(): out = lax.all_gather(both, axis, axis=0, tiled=True)  85.3 us
    all_to_all x2, waiting for transfers between devices, on_device(): lax.all_to_all(queries[block_index], 'head', split_axis=1, concat_axis=0,...  26.5 us
    split x8, local copies, waits for them, and re-layouts, rows_first(): jnp.split(out, [sum(widths[:k]) for k in range(1, len(widths))], axis=1)  26 us
    all_to_all x2, waiting for transfers between devices, on_device(): lax.all_to_all(memory_values[block_index], 'head', split_axis=1, concat_a...  22.4 us
    all_to_all x2, waiting for transfers between devices, on_device(): lax.all_to_all(memory_keys[block_index], 'head', split_axis=1, concat_axi...  20.2 us
  transfers between devices with their start and end apart: 14, of which 12 were waited for; matrix products, arithmetic and copies ran while one was open for 9% of the time, Pallas kernels for 0%

commit v1 on v0

v1 whole, which is shorter than its diff:
```python
import jax
import jax.numpy as jnp
from jax import lax
from jax.experimental import pallas as pl
from jax.experimental.pallas import tpu as pltpu
from jax.sharding import PartitionSpec as P

EPSILON = 1e-06
MESH = pl.DeviceIdType.MESH
F32 = jnp.float32
BF16 = jnp.bfloat16
GATE, UP, DOWN = 0, 1, 2
NEAR = (2, 1, 3)


def nt(a, b):
    return lax.dot_general(a, b, (((1,), (1,)), ((), ())), preferred_element_type=F32)


def nn(a, b):
    return lax.dot_general(a, b, (((1,), (0,)), ((), ())), preferred_element_type=F32)


def tn(a, b):
    return lax.dot_general(a, b, (((0,), (0,)), ((), ())), preferred_element_type=F32)


def device(x, y, z, core):
    return {"seq": x * 8 + (y // 2) * 4 + z, "head": (y % 2) * 2 + core}


def head_of(y, core):
    return 4 * (y % 2) + 2 * core + y // 2


def kernel(
    q, k, v, r, g, u, w, out, fin,
    kb, tb, qb, vb, tl, wf, st, wt, hid, ga, gb, da, db, gf, gs, r1, pf, s2, r2, wo, ob,
    tok_s, tok_r, out_s, out_r, rs1_s, rs1_r, rs2_s, rs2_r, ag1_s, ag1_r, ag2_s, ag2_r,
    fx_s, fx_r, fa1_s, fa1_r, fa2_s, fa2_r, loc,
):
    seq, hd = lax.axis_index("seq"), lax.axis_index("head")
    x, z = seq // 8, seq % 4
    y = ((seq // 4) % 2) * 2 + hd // 2
    core = hd % 2
    me = y * 2 + core
    head = head_of(y, core)
    sends = []

    def put(src, dst, ssem, rsem, where):
        copy = pltpu.make_async_remote_copy(
            src_ref=src, dst_ref=dst, send_sem=ssem, recv_sem=rsem, device_id=where, device_id_type=MESH
        )
        copy.start()
        sends.append(copy)
        return copy

    def local(src, dst, n):
        copy = pltpu.make_async_copy(src, dst, loc.at[n])
        copy.start()
        return copy

    def cols(h):
        return pl.ds(pl.multiple_of(h * 512, 512), 512)

    def rows(start, size):
        return pl.ds(pl.multiple_of(start, size), size)

    own_v = [local(v.at[c], vb.at[c], c) for c in range(2)]
    own_w = [local(m.at[y // 2], wf.at[n], 2 + n) for n, m in enumerate((g, u, w))]
    own_k = [local(k.at[c, :, cols(head)], kb.at[c, rows(me * 128, 128), :], 5 + c) for c in range(2)]
    own_q = [local(q.at[c, :, cols(head)], qb.at[c, rows(me * 128, 128), :], 7 + c) for c in range(2)]

    group = [(dy, dc) for dy in NEAR for dc in range(2)] + [(0, 1)]
    friends = [device(x, (y + dy) % 4, z, (core + dc) % 2) for dy, dc in group]
    friends += [device((x + d) % 4, y, z, core) for d in NEAR]
    friends += [device(x, y, (z + d) % 4, core) for d in NEAR]
    barrier = pltpu.get_barrier_semaphore()
    for where in friends:
        pl.semaphore_signal(barrier, inc=1, device_id=where, device_id_type=MESH)
    pl.semaphore_wait(barrier, len(friends))

    def send_tokens(c, kind, source, held):
        copies = []
        for dy, dc in group:
            y2, core2 = (y + dy) % 4, (core + dc) % 2
            n = dy * 2 + dc - 1
            copies.append(
                put(
                    source(head_of(y2, core2)),
                    held.at[c, rows(me * 128, 128), :],
                    tok_s.at[c, kind, n],
                    tok_r.at[c, kind, n],
                    device(x, y2, z, core2),
                )
            )
        return copies

    def targets(c):
        own_v[c].wait()
        for h in range(8):
            tl[c, h] = (-r[c, :, h : h + 1] * vb[c, :, h * 512 : (h + 1) * 512].astype(F32)).astype(BF16)
        tb[c, rows(me * 128, 128), :] = tl[c, head]

    got_k, got_t, got_q = [None, None], [None, None], [None, None]
    for c in range(2):
        got_k[c] = send_tokens(c, 0, lambda h: k.at[c, :, cols(h)], kb)
        targets(c)
        got_t[c] = send_tokens(c, 1, lambda h: tl.at[c, h], tb)
        got_q[c] = send_tokens(c, 2, lambda h: q.at[c, :, cols(h)], qb)

    first = (x, z)
    second = (z, x)
    share = [256 * p + 64 * first[p] + 16 * second[p] for p in range(2)]

    def along(p, phase, d):
        if (p + phase) % 2 == 0:
            return device((x + d) % 4, y, z, core)
        return device(x, y, (z + d) % 4, core)

    for n in range(3):
        own_w[n].wait()
        turned = wf[n].T
        gf[n] = turned
        wt[0, n] = turned.astype(BF16)
        for p in range(2):
            st[n, p] = gf[n, rows(share[p], 16), :]

    def reduce_out(c, m, p):
        copies = []
        for d in NEAR:
            src = gs.at[c, m, rows(256 * p + 64 * ((first[p] + d) % 4), 64), :]
            copies.append(
                put(src, r1.at[c, m, p, d - 1], rs1_s.at[c, m, p, d - 1], rs1_r.at[c, m, p, d - 1], along(p, 0, d))
            )
        return copies

    def reduce_mid(c, m, p, waits):
        for copy in waits:
            copy.wait_recv()
        total = gf[m, rows(256 * p + 64 * first[p], 64), :]
        for d in range(3):
            total = total + r1[c, m, p, d].astype(F32)
        pf[m, p] = total
        s2[c, m, p] = total.astype(BF16)
        copies = []
        for d in NEAR:
            src = s2.at[c, m, p, rows(16 * ((second[p] + d) % 4), 16), :]
            copies.append(
                put(src, r2.at[c, m, p, d - 1], rs2_s.at[c, m, p, d - 1], rs2_r.at[c, m, p, d - 1], along(p, 1, d))
            )
        return copies

    def update(c, m, p, waits):
        for copy in waits:
            copy.wait_recv()
        grad = pf[m, p, rows(16 * second[p], 16), :]
        for d in range(3):
            grad = grad + r2[c, m, p, d].astype(F32)
        old = st[m, p]
        new = old - grad
        old_norm = jnp.sqrt(jnp.sum(old * old, axis=1, keepdims=True) + EPSILON)
        new_norm = jnp.sqrt(jnp.sum(new * new, axis=1, keepdims=True) + EPSILON)
        new = new * (old_norm / new_norm)
        st[m, p] = new
        part = rows(share[p], 16)
        wt[c + 1, m, part, :] = new.astype(BF16)
        copies = []
        for d in NEAR:
            piece = wt.at[c + 1, m, part, :]
            copies.append(put(piece, piece, ag1_s.at[c, m, p, d - 1], ag1_r.at[c, m, p, d - 1], along(p, 1, d)))
        return copies

    def spread(c, m, p, waits):
        for copy in waits:
            copy.wait_recv()
        copies = []
        for d in NEAR:
            piece = wt.at[c + 1, m, rows(256 * p + 64 * first[p], 64), :]
            copies.append(put(piece, piece, ag2_s.at[c, m, p, d - 1], ag2_r.at[c, m, p, d - 1], along(p, 0, d)))
        return copies

    def both(step, c, m, waits=None):
        if waits is None:
            return [step(c, m, p) for p in range(2)]
        return [step(c, m, p, waits[p]) for p in range(2)]

    def arrived(copies):
        for part in copies:
            for copy in part:
                copy.wait_recv()

    def forward(c):
        own_k[c].wait()
        for copy in got_k[c]:
            copy.wait_recv()

        def block(i, _):
            part = rows(i * 256, 256)
            keys = kb[c, part, :]
            a = nt(keys, wt[c, GATE])
            b = nt(keys, wt[c, UP])
            s = jax.nn.sigmoid(a)
            act = a * s
            hid[part, :] = (act * b).astype(BF16)
            ga[part, :] = b * s * (1.0 + a * (1.0 - s))
            gb[part, :] = act
            return 0

        lax.fori_loop(0, 4, block, 0)

    def grad_half(c, m, p, left, right):
        res = tn(left[:, 256 * p : 256 * (p + 1)], right)
        gf[m, 256 * p : 256 * (p + 1), :] = res
        gs[c, m, 256 * p : 256 * (p + 1), :] = res.astype(BF16)
        return reduce_out(c, m, p)

    def deltas(c):
        def block(i, _):
            part = rows(i * 256, 256)
            dh = nn(tb[c, part, :], wt[c, DOWN])
            da[part, :] = (dh * ga[part, :]).astype(BF16)
            db[part, :] = (dh * gb[part, :]).astype(BF16)
            return 0

        lax.fori_loop(0, 4, block, 0)

    kept = []

    def apply_block(c, dy):
        y2 = (y + dy) % 4
        part = rows(256 * y2, 256)
        queries = qb[c, part, :]
        p = nt(queries, wt[c + 1, GATE])
        u2 = nt(queries, wt[c + 1, UP])
        hidden = (p * jax.nn.sigmoid(p) * u2).astype(BF16)
        ob[c, part, :] = nt(hidden, wt[c + 1, DOWN]).astype(BF16)
        copies = []
        for dc in range(2):
            core2 = (core + dc) % 2
            tile = ob.at[c, rows(256 * y2 + 128 * core2, 128), :]
            place = out.at[c, :, cols(head)]
            if dy == 0 and dc == 0:
                kept.append(local(tile, place, 9 + c))
            else:
                n = dy * 2 + dc - 1
                copies.append(put(tile, place, out_s.at[c, n], out_r.at[c, n], device(x, y2, z, core2)))
        return copies

    got_out = []

    def apply_all(c):
        own_q[c].wait()
        for copy in got_q[c]:
            copy.wait_recv()
        for dy in NEAR + (0,):
            got_out.extend(apply_block(c, dy))

    def other_exchange():
        copies = []
        for p in range(2):
            part = rows(share[p], 16)
            copies.append(
                put(wt.at[2, :, part, :], wo.at[:, part, :], fx_s.at[p], fx_r.at[p], device(x, (y + 2) % 4, z, core))
            )
        return copies

    def other_first(waits):
        copies = []
        for p in range(2):
            waits[p].wait_recv()
            piece = wo.at[:, rows(share[p], 16), :]
            copies.append(
                [put(piece, piece, fa1_s.at[p, d - 1], fa1_r.at[p, d - 1], along(p, 1, d)) for d in NEAR]
            )
        return copies

    def other_second(waits):
        copies = []
        for p in range(2):
            for copy in waits[p]:
                copy.wait_recv()
            piece = wo.at[:, rows(256 * p + 64 * first[p], 64), :]
            copies.append(
                [put(piece, piece, fa2_s.at[p, d - 1], fa2_r.at[p, d - 1], along(p, 0, d)) for d in NEAR]
            )
        return copies

    for c in range(2):
        forward(c)
        for copy in got_t[c]:
            copy.wait_recv()
        w1 = [grad_half(c, DOWN, p, tb.at[c], hid[...]) for p in range(2)]
        deltas(c)
        g1 = [grad_half(c, GATE, p, da, kb[c]) for p in range(2)]
        w2 = both(reduce_mid, c, DOWN, w1)
        u1 = [grad_half(c, UP, p, db, kb[c]) for p in range(2)]
        g2 = both(reduce_mid, c, GATE, g1)
        w3 = both(update, c, DOWN, w2)
        if c == 1:
            apply_all(0)
        u2 = both(reduce_mid, c, UP, u1)
        g3 = both(update, c, GATE, g2)
        w4 = both(spread, c, DOWN, w3)
        u3 = both(update, c, UP, u2)
        if c == 1:
            fx = other_exchange()
        g4 = both(spread, c, GATE, g3)
        u4 = both(spread, c, UP, u3)
        if c == 1:
            f1 = other_first(fx)
        arrived(g4)
        arrived(u4)
        arrived(w4)
    apply_all(1)
    f2 = other_second(f1)
    for n in range(3):
        fin[n, y // 2] = wt[2, n].astype(F32).T.astype(BF16)
    arrived(f2)
    for n in range(3):
        fin[n, 1 - y // 2] = wo[n].astype(F32).T.astype(BF16)
    for copy in got_out:
        copy.wait_recv()
    for copy in kept:
        copy.wait()
    for copy in sends:
        copy.wait_send()


def on_device(queries, memory_keys, memory_values, rates, fast_gate, fast_up, fast_down):
    anywhere = pl.BlockSpec(memory_space=pl.ANY)
    inside = pl.BlockSpec(memory_space=pltpu.VMEM)
    dma = pltpu.SemaphoreType.DMA
    tokens = pltpu.VMEM((2, 1024, 512), BF16)
    plain = pltpu.VMEM((1024, 512), BF16)
    wide = pltpu.VMEM((1024, 512), F32)
    out, fin = pl.pallas_call(
        kernel,
        name="fast_weights",
        out_shape=(
            jax.ShapeDtypeStruct((2, 128, 4096), BF16),
            jax.ShapeDtypeStruct((3, 2, 512, 512), BF16),
        ),
        in_specs=[anywhere, anywhere, anywhere, inside, anywhere, anywhere, anywhere],
        out_specs=(anywhere, inside),
        scratch_shapes=[
            tokens, tokens, tokens,
            pltpu.VMEM((2, 128, 4096), BF16),
            pltpu.VMEM((2, 8, 128, 512), BF16),
            pltpu.VMEM((3, 512, 512), F32),
            pltpu.VMEM((3, 2, 16, 512), F32),
            pltpu.VMEM((3, 3, 512, 512), BF16),
            plain, wide, wide, plain, plain,
            pltpu.VMEM((3, 512, 512), F32),
            pltpu.VMEM((2, 3, 512, 512), BF16),
            pltpu.VMEM((2, 3, 2, 3, 64, 512), BF16),
            pltpu.VMEM((3, 2, 64, 512), F32),
            pltpu.VMEM((2, 3, 2, 64, 512), BF16),
            pltpu.VMEM((2, 3, 2, 3, 16, 512), BF16),
            pltpu.VMEM((3, 512, 512), BF16),
            tokens,
            dma((2, 3, 7)), dma((2, 3, 7)),
            dma((2, 7)), dma((2, 7)),
            dma((2, 3, 2, 3)), dma((2, 3, 2, 3)),
            dma((2, 3, 2, 3)), dma((2, 3, 2, 3)),
            dma((2, 3, 2, 3)), dma((2, 3, 2, 3)),
            dma((2, 3, 2, 3)), dma((2, 3, 2, 3)),
            dma((2,)), dma((2,)),
            dma((2, 3)), dma((2, 3)),
            dma((2, 3)), dma((2, 3)),
            dma((11,)),
        ],
        compiler_params=pltpu.CompilerParams(
            collective_id=0, has_side_effects=True, vmem_limit_bytes=60 << 20
        ),
    )(queries, memory_keys, memory_values, rates, fast_gate, fast_up, fast_down)
    state = fin.astype(F32)
    return out, state[0], state[1], state[2]


def solution(mesh):
    tokens = P(None, ("seq", "head"), None)
    heads = P("head", None, None)
    return jax.shard_map(
        on_device,
        mesh=mesh,
        in_specs=(tokens, tokens, tokens, tokens, heads, heads, heads),
        out_specs=(tokens, heads, heads, heads),
        check_vma=False,
    )
```

time: 859 us -> 125 us (0.15); the launches traced: 849 us -> 125 us
  waiting for transfers between devices: 636 us -> 0 us
  Pallas kernels: 0 us -> 116 us
  local copies, waits for them, and re-layouts: 90.4 us -> 5.68 us
  starting transfers between devices: 50 us -> 0 us
  matrix products: 40.7 us -> 0 us
  other arithmetic: 17.3 us -> 2.75 us
  between operations: 14.6 us -> 0.66 us
    reduce_scatter x2 -> x0, waiting for transfers between devices: 469 us -> none  [side_by_side(): lax.psum_scatter(both, axis, scatter_dimension=dim, tiled=True)]
    pallas_call x0 -> x1, Pallas kernels: none -> 116 us  [on_device(): pl.pallas_call(kernel, name='fast_weights', out_shape=(jax.ShapeDtypeStru...]
    all_gather x2 -> x0, waiting for transfers between devices: 85.3 us -> none  [rows_first(): out = lax.all_gather(both, axis, axis=0, tiled=True)]
    all_to_all x10 -> x0, waiting for transfers between devices: 82 us -> none  [the longest x2 26.5 us: on_device(): lax.all_to_all(queries[block_index], 'head', split_axis=1, concat_axis=0,...]
    all_to_all x10 -> x0, starting transfers between devices: 49.7 us -> none  [the longest x2 11.5 us: on_device(): lax.all_to_all(queries[block_index], 'head', split_axis=1, concat_axis=0,...]
    dot_general x16 -> x0, matrix products: 40.7 us -> none  [the longest x2 8.44 us: apply_head(): jnp.dot(hidden, down_weight.astype(jnp.bfloat16), preferred_element_type=...]
    split x8 -> x0, local copies, waits for them, and re-layouts: 26 us -> none  [rows_first(): jnp.split(out, [sum(widths[:k]) for k in range(1, len(widths))], axis=1)]
    all_to_all x16 -> x0, local copies, waits for them, and re-layouts: 22.2 us -> none  [the longest x4 8.26 us: on_device(): lax.all_to_all(queries[block_index], 'head', split_axis=1, concat_axis=0,...]
  transfers between devices with their start and end apart: 14 -> 0, of which waited for: 12 -> 0; matrix products, arithmetic and copies ran while one was open for 9% -> 0% of each run, Pallas kernels for 0% -> 0%
where the time goes in v1:
time: 125 us
  Pallas kernels  116 us (93%)
  local copies, waits for them, and re-layouts  5.68 us (5%)
  other arithmetic  2.75 us (2%)
    pallas_call x1, Pallas kernels, on_device(): pl.pallas_call(kernel, name='fast_weights', out_shape=(jax.ShapeDtypeStru...  116 us
    squeeze x1, local copies, waits for them, and re-layouts, on_device(): return (out, state[0], state[1], state[2])  2.87 us
    unnamed x4, local copies, waits for them, and re-layouts  2.81 us
    convert_element_type x1, other arithmetic, on_device(): state = fin.astype(F32)  2.75 us

profile of v1, /device:TPU:1, one launch (start us, length us, event | category | flops | bytes accessed | tf_op | source)
XLA Modules:
  0.0 124.8 jit_solution(17528248687877622584)
XLA Ops:
  0.6 1.5 %copy.11.r = f32[2,128,8]{2,1,0:T(8,128)} copy(f32[2,128,8]{1,2,0:T(8,128)} %param.10) | data formatting | bytes 16384 | tf_op args[3]
  2.1 115.7 %fast_weights.1 = (bf16[2,128,4096]{2,1,0:T(8,128)(2,1)}, bf16[3,2,512,512]{3,2,1,0:T(8,128)(2,1)}) custom-call(bf16[2,128,4096]{2,1,0:T(8,128)(2,1)} %q.1, bf16[2,128,4096]{2,1,0:T(8,128)(2,1)} %k.1, bf16[2,128,4096]{2,1,0:T(8,128)(2,1)} %v.1, f32[2,128,8]{2,1,0:T(8,128)} %copy.11.r, f32[2,512,512]{2,1,0:T(8,128)} %g.1, f32[2,512,512]{2,1,0:T(8,128)} %u.1, ...), custom_call_target="tpu_custom_call" | custom-call | tf_op jit(solution)/shard_map/fast_weights/pallas_call | solution.py:337
  117.9 2.8 %convert_element_type.3 = f32[3,2,512,512]{3,2,1,0:T(8,128)S(1)} convert(bf16[3,2,512,512]{3,2,1,0:T(8,128)(2,1)} %get-tuple-element.7) | non-fusion elementwise | flops 1572864 | bytes 9437184 | tf_op jit(solution)/shard_map/convert_element_type | solution.py:377
  120.6 0.0 copy-start
  120.6 2.9 %slice_bitcast_fusion = (f32[2,512,512]{2,1,0:T(8,128)}, f32[2,512,512]{2,1,0:T(8,128)}, f32[2,512,512]{2,1,0:T(8,128)}) fusion(f32[3,2,512,512]{3,2,1,0:T(8,128)S(1)} %convert_element_type.3), kind=kLoop, calls=%fused_computation | loop fusion | bytes 12582912 | tf_op jit(solution)/shard_map/squeeze | solution.py:378
  123.5 0.0 copy-done
  123.5 1.3 %copy.13 = bf16[2,128,4096]{2,1,0:T(8,128)(2,1)} copy(bf16[2,128,4096]{2,1,0:T(8,128)(2,1)S(1)} %copy-done) | data formatting | bytes 4194304
Async XLA Ops:
  120.6 2.9 %copy-start = (bf16[2,128,4096]{2,1,0:T(8,128)(2,1)S(1)}, bf16[2,128,4096]{2,1,0:T(8,128)(2,1)}, u32[]{:S(2)}) copy-start(bf16[2,128,4096]{2,1,0:T(8,128)(2,1)} %get-tuple-element.15) | copy-start | bytes 6291460

commit v2 on v1

--- a/solution.py
+++ b/solution.py
@@ -97,9 +97,10 @@
         return copies
 
     def targets(c):
+        rate = r[c].T
         own_v[c].wait()
         for h in range(8):
-            tl[c, h] = (-r[c, :, h : h + 1] * vb[c, :, h * 512 : (h + 1) * 512].astype(F32)).astype(BF16)
+            tl[c, h] = (-rate[:, h : h + 1] * vb[c, :, h * 512 : (h + 1) * 512].astype(F32)).astype(BF16)
         tb[c, rows(me * 128, 128), :] = tl[c, head]
 
     got_k, got_t, got_q = [None, None], [None, None], [None, None]
@@ -286,6 +287,16 @@
             )
         return copies
 
+    def ready(c):
+        if c == 1:
+            own_q[0].wait()
+            for copy in got_q[0]:
+                copy.wait_recv()
+
+    def piece_of(c, dy):
+        if c == 1:
+            got_out.extend(apply_block(0, dy))
+
     for c in range(2):
         forward(c)
         for copy in got_t[c]:
@@ -295,12 +306,15 @@
         g1 = [grad_half(c, GATE, p, da, kb[c]) for p in range(2)]
         w2 = both(reduce_mid, c, DOWN, w1)
         u1 = [grad_half(c, UP, p, db, kb[c]) for p in range(2)]
+        ready(c)
         g2 = both(reduce_mid, c, GATE, g1)
+        piece_of(c, 2)
         w3 = both(update, c, DOWN, w2)
-        if c == 1:
-            apply_all(0)
+        piece_of(c, 1)
         u2 = both(reduce_mid, c, UP, u1)
+        piece_of(c, 3)
         g3 = both(update, c, GATE, g2)
+        piece_of(c, 0)
         w4 = both(spread, c, DOWN, w3)
         u3 = both(update, c, UP, u2)
         if c == 1:
@@ -373,9 +387,8 @@
         compiler_params=pltpu.CompilerParams(
             collective_id=0, has_side_effects=True, vmem_limit_bytes=60 << 20
         ),
-    )(queries, memory_keys, memory_values, rates, fast_gate, fast_up, fast_down)
-    state = fin.astype(F32)
-    return out, state[0], state[1], state[2]
+    )(queries, memory_keys, memory_values, jnp.swapaxes(rates, 1, 2), fast_gate, fast_up, fast_down)
+    return out, *[lax.index_in_dim(fin, n, 0, keepdims=False).astype(F32) for n in range(3)]
 
 
 def solution(mesh):

time: 125 us -> 122 us (0.976)
  local copies, waits for them, and re-layouts: 5.68 us -> 1.32 us
  other arithmetic: 2.75 us -> 5 us
    squeeze x1 -> x0, local copies, waits for them, and re-layouts: 2.87 us -> none  [on_device(): return (out, state[0], state[1], state[2])]
    convert_element_type x1, other arithmetic: 2.75 us -> 5 us  [on_device(): lax.index_in_dim(fin, n, 0, keepdims=False).astype(F32)]
    unnamed x4 -> x3, local copies, waits for them, and re-layouts: 2.81 us -> 1.32 us
where the time goes in v2:
time: 122 us
  Pallas kernels  115 us (94%)
  other arithmetic  5 us (4%)
  local copies, waits for them, and re-layouts  1.32 us (1%)
    pallas_call x1, Pallas kernels, on_device(): pl.pallas_call(kernel, name='fast_weights', out_shape=(jax.ShapeDtypeStru...  115 us
    convert_element_type x1, other arithmetic, on_device(): lax.index_in_dim(fin, n, 0, keepdims=False).astype(F32)  5 us

profile of v2, /device:TPU:1, one launch (start us, length us, event | category | flops | bytes accessed | tf_op | source)
XLA Modules:
  0.0 121.6 jit_solution(17263391358218484946)
XLA Ops:
  0.6 114.6 %fast_weights.1 = (bf16[2,128,4096]{2,1,0:T(8,128)(2,1)}, bf16[3,2,512,512]{3,2,1,0:T(8,128)(2,1)}) custom-call(bf16[2,128,4096]{2,1,0:T(8,128)(2,1)} %q.1, bf16[2,128,4096]{2,1,0:T(8,128)(2,1)} %k.1, bf16[2,128,4096]{2,1,0:T(8,128)(2,1)} %v.1, f32[2,8,128]{2,1,0:T(8,128)} %bitcast.10, f32[2,512,512]{2,1,0:T(8,128)} %g.1, f32[2,512,512]{2,1,0:T(8,128)} %u.1, ...), custom_call_target="tpu_custom_call" | custom-call | tf_op jit(solution)/shard_map/fast_weights/pallas_call | solution.py:351
  115.3 0.0 copy-start
  115.3 5.0 %bitcast_convert_fusion = (f32[2,512,512]{2,1,0:T(8,128)}, f32[2,512,512]{2,1,0:T(8,128)}, f32[2,512,512]{2,1,0:T(8,128)}) fusion(bf16[3,2,512,512]{3,2,1,0:T(8,128)(2,1)} %get-tuple-element.7), kind=kLoop, calls=%fused_computation | loop fusion | flops 1572864 | bytes 9437184 | tf_op jit(solution)/shard_map/convert_element_type | solution.py:391
  120.3 0.0 copy-done
  120.3 1.3 %copy.12 = bf16[2,128,4096]{2,1,0:T(8,128)(2,1)} copy(bf16[2,128,4096]{2,1,0:T(8,128)(2,1)S(1)} %copy-done) | data formatting | bytes 4194304
Async XLA Ops:
  115.3 5.0 %copy-start = (bf16[2,128,4096]{2,1,0:T(8,128)(2,1)S(1)}, bf16[2,128,4096]{2,1,0:T(8,128)(2,1)}, u32[]{:S(2)}) copy-start(bf16[2,128,4096]{2,1,0:T(8,128)(2,1)} %get-tuple-element.15) | copy-start | bytes 6291460

commit v3 on v2

--- a/solution.py
+++ b/solution.py
@@ -108,6 +108,7 @@
         got_k[c] = send_tokens(c, 0, lambda h: k.at[c, :, cols(h)], kb)
         targets(c)
         got_t[c] = send_tokens(c, 1, lambda h: tl.at[c, h], tb)
+    for c in range(2):
         got_q[c] = send_tokens(c, 2, lambda h: q.at[c, :, cols(h)], qb)
 
     first = (x, z)

time: 122 us -> 119 us (0.975)
  Pallas kernels: 115 us -> 111 us
    pallas_call x1, Pallas kernels: 115 us -> 111 us  [on_device(): pl.pallas_call(kernel, name='fast_weights', out_shape=(jax.ShapeDtypeStru...]
where the time goes in v3:
time: 119 us; the launch traced here: 118 us
  Pallas kernels  111 us (93%)
  other arithmetic  5 us (4%)
  local copies, waits for them, and re-layouts  1.32 us (1%)
    pallas_call x1, Pallas kernels, on_device(): pl.pallas_call(kernel, name='fast_weights', out_shape=(jax.ShapeDtypeStru...  111 us
    convert_element_type x1, other arithmetic, on_device(): lax.index_in_dim(fin, n, 0, keepdims=False).astype(F32)  5 us

profile of v3, /device:TPU:1, one launch (start us, length us, event | category | flops | bytes accessed | tf_op | source)
XLA Modules:
  0.0 118.4 jit_solution(16983690733444507163)
XLA Ops:
  0.6 111.4 %fast_weights.1 = (bf16[2,128,4096]{2,1,0:T(8,128)(2,1)}, bf16[3,2,512,512]{3,2,1,0:T(8,128)(2,1)}) custom-call(bf16[2,128,4096]{2,1,0:T(8,128)(2,1)} %q.1, bf16[2,128,4096]{2,1,0:T(8,128)(2,1)} %k.1, bf16[2,128,4096]{2,1,0:T(8,128)(2,1)} %v.1, f32[2,8,128]{2,1,0:T(8,128)} %bitcast.10, f32[2,512,512]{2,1,0:T(8,128)} %g.1, f32[2,512,512]{2,1,0:T(8,128)} %u.1, ...), custom_call_target="tpu_custom_call" | custom-call | tf_op jit(solution)/shard_map/fast_weights/pallas_call | solution.py:352
  112.1 0.0 copy-start
  112.1 5.0 %bitcast_convert_fusion = (f32[2,512,512]{2,1,0:T(8,128)}, f32[2,512,512]{2,1,0:T(8,128)}, f32[2,512,512]{2,1,0:T(8,128)}) fusion(bf16[3,2,512,512]{3,2,1,0:T(8,128)(2,1)} %get-tuple-element.7), kind=kLoop, calls=%fused_computation | loop fusion | flops 1572864 | bytes 9437184 | tf_op jit(solution)/shard_map/convert_element_type | solution.py:392
  117.1 0.0 copy-done
  117.1 1.3 %copy.12 = bf16[2,128,4096]{2,1,0:T(8,128)(2,1)} copy(bf16[2,128,4096]{2,1,0:T(8,128)(2,1)S(1)} %copy-done) | data formatting | bytes 4194304
Async XLA Ops:
  112.1 5.0 %copy-start = (bf16[2,128,4096]{2,1,0:T(8,128)(2,1)S(1)}, bf16[2,128,4096]{2,1,0:T(8,128)(2,1)}, u32[]{:S(2)}) copy-start(bf16[2,128,4096]{2,1,0:T(8,128)(2,1)} %get-tuple-element.15) | copy-start | bytes 6291460
